TPU v7x, 512 devices: a whole 4x8x8 slice. The times are simulated.
512 devices in a mesh: dp: 64 (over z_lo, y, core), mp: 8 (over x, z_hi).
Axes of the slice: x: 4, y: 8, z: 8 (z_hi: 2, z_lo: 4; z = z_hi * 4 + z_lo), core: 2. Of those that a mesh axis runs over, the one named last changes fastest.
Arguments:
- activations: bfloat16 [65536, 4096], P('dp', 'mp'), may hold values from -6 to 6
- out_grad: bfloat16 [65536, 14336], P('dp', 'mp'), may hold values from -0.0234375 to 0.0234375
- tile_list: int32 [8, 64, 2], P('mp'), may hold values from 0 to 111, as said below
- tile_count: int32 [8], P('mp'), may hold values from 32 to 64, as said below
Outputs:
- grad_tiles: float32 [8, 64, 128, 128], P('mp', 'dp')
Inputs may be any that keep to these rules, and one draw needn't show every extreme that they name: `tile_list`: in shard c the 64 entries name distinct blocks; the block row lies in 0 to 31 and the block column in c * 14 to (c + 1) * 14 - 1. `tile_count`: some shard has all 64 slots live.
All inputs are finite; a program needn't handle non-finite values.
Results may differ from a plain program's by a relative error of at most 0.0003.
Values may be sent and summed in bfloat16 or wider, within the bound.
A program may use at most 128 MiB of HBM per device.

v0:
```python
import math

import jax
import jax.numpy as jnp
from jax import lax
from jax.sharding import PartitionSpec as P

D = 4096
BLK = 128


def on_device(activations, out_grad, tile_list, tile_count):
    gathered = lax.all_gather(activations, "mp", axis=1, tiled=True)
    token_count = gathered.shape[0]
    slot_total = tile_list.shape[1]
    col_blocks = out_grad.shape[1] // BLK
    row_ids = tile_list[0, :, 0]
    col_ids = tile_list[0, :, 1] - lax.axis_index("mp") * col_blocks
    active = (jnp.arange(slot_total, dtype=jnp.int32) < tile_count[0]).astype(jnp.float32)
    act_blocks = gathered.reshape(token_count, D // BLK, BLK)
    grad_blocks = out_grad.reshape(token_count, col_blocks, BLK)

    def group_product(indices):
        act_sel = jnp.take(act_blocks, indices[0], axis=1)
        grad_sel = jnp.take(grad_blocks, indices[1], axis=1)
        return jnp.einsum("tkr,tkc->krc", act_sel, grad_sel, preferred_element_type=jnp.float32)

    count = row_ids.shape[0]
    group_size = math.gcd(count, 16)
    result = lax.map(
        group_product, (row_ids.reshape(-1, group_size), col_ids.reshape(-1, group_size))
    )
    summed = lax.psum_scatter(
        result.reshape(count, BLK, BLK) * active[:, None, None],
        "dp",
        scatter_dimension=0,
        tiled=True,
    )
    return summed[None]


def solution(mesh):
    placed = (P("dp", "mp"), P("dp", "mp"), P("mp", None, None), P("mp"))
    return jax.shard_map(
        on_device, mesh=mesh, in_specs=placed, out_specs=P("mp", "dp", None, None), check_vma=False
    )
```

profile of v0, /device:TPU:2, one launch (start us, length us, event | category | flops | bytes accessed | tf_op | source)
XLA Modules:
  0.0 573.7 jit_solution(4600374275060258306)
XLA Ops:
  6.5 0.0 all-gather.2.cloned.1.call-start
  6.5 2.3 copy.11
  8.8 0.0 all-gather.2.cloned.1.call-update
  8.8 0.0 reduce-scatter.2.cloned.1.call-start
  8.9 0.8 subtract_reduce_fusion
  9.7 0.1 reshape_squeeze.3
  9.8 0.1 sub.12
  9.8 5.9 %copy.12 = bf16[1024,1792]{0,1:T(8,128)(2,1)} copy(bf16[1024,1792]{1,0:T(8,128)(2,1)} %param.7) | data formatting | bytes 7340032 | tf_op args[1]
  15.8 5.9 %copy.14 = bf16[1024,14,128]{2,0,1:T(8,128)(2,1)} copy(bf16[1024,14,128]{0,2,1:T(8,128)(2,1)} %bitcast.49) | data formatting | bytes 7340032 | tf_op jit(solution)/shard_map/while | solution.py:30
  22.3 171.0 %all-gather.2.cloned.1.call-done = bf16[1024,4096]{0,1:T(8,128)(2,1)} async-done(((bf16[1024,512]{0,1:T(8,128)(2,1)}), bf16[1024,4096]{0,1:T(8,128)(2,1)}) %all-gather.2.cloned.1.call-update) | async-done | bytes 8388624 | tf_op jit(solution)/shard_map/all_gather | solution.py:13
  193.3 11.9 %copy.13 = bf16[1024,32,128]{2,0,1:T(8,128)(2,1)} copy(bf16[1024,32,128]{0,2,1:T(8,128)(2,1)} %bitcast.50) | data formatting | bytes 16777216 | tf_op jit(solution)/shard_map/while | solution.py:30
  205.3 70.6 %while.10 = (s32[]{:T(128)}, f32[4,16,128,128]{3,2,1,0:T(8,128)}, s32[4,16]{1,0:T(4,128)S(1)}, bf16[1024,32,128]{2,0,1:T(8,128)(2,1)}, s32[4,16]{1,0:T(4,128)S(1)}, /*index=5*/bf16[1024,14,128]{2,0,1:T(8,128)(2,1)}, s32[]{:T(128)}) while((s32[]{:T(128)}, f32[4,16,128,128]{3,2,1,0:T(8,128)}, s32[4,16]{1,0:T(4,128)S(1)}, ...), condition=%wide.region_1.2_spmd, body=%wide.region_0.1_spmd.sunk | while | flops 541067584 | bytes 26223892 | solution.py:30
  205.3 5.1 gather_fusion
  210.4 6.4 %gather_fusion.1 = bf16[16,1024,128]{2,1,0:T(8,128)(2,1)} fusion(bf16[1024,32,128]{2,0,1:T(8,128)(2,1)} %get-tuple-element.130, s32[1024]{0:T(1024)S(1)} %pad_clamp_fusion.5), kind=kCustom, calls=%fused_computation.clone.1 | custom fusion | bytes 8388672 | tf_op jit(solution)/shard_map/while/body/eval_jaxpr/jit(_take)/gather | solution.py:24
  216.8 6.1 %fusion.28 = f32[4,16,128,128]{3,2,1,0:T(8,128)} fusion(f32[4,16,128,128]{3,2,1,0:T(8,128)} %get-tuple-element.121, s32[]{:T(128)} %get-tuple-element.120, bf16[16,1024,128]{2,1,0:T(8,128)(2,1)} %gather_fusion, pred[16]{0:T(512)(128)(4,1)S(1)} %get-tuple-element.110, bf16[16,1024,128]{2,1,0:T(8,128)(2,1)} %gather_fusion.1, ...), kind=kOutput, calls=%fused_computation.11.clone.1 | convolution fusion | flops 541065216 | bytes 9437728 | tf_op jit(solution)/shard_map/while/body/eval_jaxpr/tkr,tkc->krc/dot_general | solution.py:26
  222.9 5.1 gather_fusion
  228.0 6.4 %gather_fusion.1 = bf16[16,1024,128]{2,1,0:T(8,128)(2,1)} fusion(bf16[1024,32,128]{2,0,1:T(8,128)(2,1)} %get-tuple-element.130, s32[1024]{0:T(1024)S(1)} %pad_clamp_fusion.5), kind=kCustom, calls=%fused_computation.clone.1 | custom fusion | bytes 8388672 | tf_op jit(solution)/shard_map/while/body/eval_jaxpr/jit(_take)/gather | solution.py:24
  234.4 6.1 %fusion.28 = f32[4,16,128,128]{3,2,1,0:T(8,128)} fusion(f32[4,16,128,128]{3,2,1,0:T(8,128)} %get-tuple-element.121, s32[]{:T(128)} %get-tuple-element.120, bf16[16,1024,128]{2,1,0:T(8,128)(2,1)} %gather_fusion, pred[16]{0:T(512)(128)(4,1)S(1)} %get-tuple-element.110, bf16[16,1024,128]{2,1,0:T(8,128)(2,1)} %gather_fusion.1, ...), kind=kOutput, calls=%fused_computation.11.clone.1 | convolution fusion | flops 541065216 | bytes 9437728 | tf_op jit(solution)/shard_map/while/body/eval_jaxpr/tkr,tkc->krc/dot_general | solution.py:26
  240.6 5.1 gather_fusion
  245.7 6.4 %gather_fusion.1 = bf16[16,1024,128]{2,1,0:T(8,128)(2,1)} fusion(bf16[1024,32,128]{2,0,1:T(8,128)(2,1)} %get-tuple-element.130, s32[1024]{0:T(1024)S(1)} %pad_clamp_fusion.5), kind=kCustom, calls=%fused_computation.clone.1 | custom fusion | bytes 8388672 | tf_op jit(solution)/shard_map/while/body/eval_jaxpr/jit(_take)/gather | solution.py:24
  252.1 6.1 %fusion.28 = f32[4,16,128,128]{3,2,1,0:T(8,128)} fusion(f32[4,16,128,128]{3,2,1,0:T(8,128)} %get-tuple-element.121, s32[]{:T(128)} %get-tuple-element.120, bf16[16,1024,128]{2,1,0:T(8,128)(2,1)} %gather_fusion, pred[16]{0:T(512)(128)(4,1)S(1)} %get-tuple-element.110, bf16[16,1024,128]{2,1,0:T(8,128)(2,1)} %gather_fusion.1, ...), kind=kOutput, calls=%fused_computation.11.clone.1 | convolution fusion | flops 541065216 | bytes 9437728 | tf_op jit(solution)/shard_map/while/body/eval_jaxpr/tkr,tkc->krc/dot_general | solution.py:26
  258.2 5.1 gather_fusion
  263.3 6.4 %gather_fusion.1 = bf16[16,1024,128]{2,1,0:T(8,128)(2,1)} fusion(bf16[1024,32,128]{2,0,1:T(8,128)(2,1)} %get-tuple-element.130, s32[1024]{0:T(1024)S(1)} %pad_clamp_fusion.5), kind=kCustom, calls=%fused_computation.clone.1 | custom fusion | bytes 8388672 | tf_op jit(solution)/shard_map/while/body/eval_jaxpr/jit(_take)/gather | solution.py:24
  269.7 6.1 %fusion.28 = f32[4,16,128,128]{3,2,1,0:T(8,128)} fusion(f32[4,16,128,128]{3,2,1,0:T(8,128)} %get-tuple-element.121, s32[]{:T(128)} %get-tuple-element.120, bf16[16,1024,128]{2,1,0:T(8,128)(2,1)} %gather_fusion, pred[16]{0:T(512)(128)(4,1)S(1)} %get-tuple-element.110, bf16[16,1024,128]{2,1,0:T(8,128)(2,1)} %gather_fusion.1, ...), kind=kOutput, calls=%fused_computation.11.clone.1 | convolution fusion | flops 541065216 | bytes 9437728 | tf_op jit(solution)/shard_map/while/body/eval_jaxpr/tkr,tkc->krc/dot_general | solution.py:26
  275.8 4.5 bitcast_multiply_fusion
  280.3 0.0 reduce-scatter.2.cloned.1.call-update
  280.3 286.6 %reduce-scatter.2.cloned.1.call-done = f32[1,128,128]{2,1,0:T(8,128)} async-done(((f32[64,128,128]{2,1,0:T(8,128)}), f32[1,128,128]{2,1,0:T(8,128)}) %reduce-scatter.2.cloned.1.call-update) | async-done | bytes 65552 | tf_op jit(solution)/shard_map/reduce_scatter | solution.py:33
  (18 shorter events, 0.1 us)
Async XLA Ops:
  6.5 186.8 %all-gather.2.cloned.1.call-start = ((), (), s32[]{:S(2)}) async-start(), calls=%async_computation.1 | async-start | bytes 9437184 | tf_op jit(solution)/shard_map/all_gather | solution.py:13
  8.8 558.0 %reduce-scatter.2.cloned.1.call-start = ((), (), s32[]{:S(2)}) async-start(), calls=%async_computation.2 | async-start | bytes 4259840 | tf_op jit(solution)/shard_map/reduce_scatter | solution.py:33
Sparse Core Ops, SparseCore 0:
  10.5 182.7 all-gather.1
  280.4 286.3 reduce-scatter.1
where the time goes:
time: 575 us; the launch traced here: 574 us
  waiting for transfers between devices  458 us (80%)
  local copies, waits for them, and re-layouts  72.2 us (13%)
  matrix products  24.5 us (4%)
  between operations  14.1 us (2%)
    reduce_scatter x1, waiting for transfers between devices, on_device(): lax.psum_scatter(result.reshape(count, BLK, BLK) * active[:, None, None],...  287 us
    all_gather x1, waiting for transfers between devices, on_device(): gathered = lax.all_gather(activations, 'mp', axis=1, tiled=True)  171 us
    gather x4, local copies, waits for them, and re-layouts, group_product(): act_sel = jnp.take(act_blocks, indices[0], axis=1)  25.6 us
    dot_general x4, matrix products, group_product(): jnp.einsum('tkr,tkc->krc', act_sel, grad_sel, preferred_element_type=jnp....  24.5 us
    gather x4, local copies, waits for them, and re-layouts, group_product(): grad_sel = jnp.take(grad_blocks, indices[1], axis=1)  20.3 us
    while x2, local copies, waits for them, and re-layouts, on_device(): lax.map(group_product, (row_ids.reshape(-1, group_size), col_ids.reshape(...  17.8 us
  transfers between devices with their start and end apart: 2, of which 2 were waited for; matrix products, arithmetic and copies ran while one was open for 2% of the time, Pallas kernels for 0%

commit v1 on v0

v1 whole, which is shorter than its diff:
```python
import jax
import jax.numpy as jnp
from jax import lax
from jax.experimental import pallas as pl
from jax.experimental.pallas import tpu as pltpu
from jax.sharding import PartitionSpec as P

MESH = pl.DeviceIdType.MESH
BLK = 128
NX, NY, NZL = 4, 8, 4
T = 4


def rem(a, b):
    return lax.rem(a, jnp.int32(b))


def div(a, b):
    return lax.div(a, jnp.int32(b))


def kernel(tl, act, grad, out, *scratch):
    gath = scratch[:T]
    gbuf, acc, crecv, yrp, yrm, zrecv, lsem, gsem, ssem, rsem = scratch[T:]
    tokens, feats = act.shape
    ch = tokens // T
    hf = ch // 2
    cols = grad.shape[1] // BLK
    per = feats // BLK

    dp, mp = lax.axis_index("dp"), lax.axis_index("mp")
    core, y, zl = rem(dp, 2), rem(div(dp, 2), NY), div(dp, 2 * NY)
    x, zh = div(mp, 2), rem(mp, 2)

    def dev(x_, y_, zl_, zh_, core_):
        return ((zl_ * NY + y_) * 2 + core_, x_ * 2 + zh_)

    xr, xl = rem(x + 1, NX), rem(x + NX - 1, NX)
    right, left = dev(xr, y, zl, zh, core), dev(xl, y, zl, zh, core)
    across = dev(x, y, zl, 1 - zh, core)
    twin = dev(x, y, zl, zh, 1 - core)
    up, down = dev(x, rem(y + 1, NY), zl, zh, core), dev(x, rem(y + NY - 1, NY), zl, zh, core)

    loc_a = []
    for t in range(T):
        for b in range(per):
            c = pltpu.make_async_copy(
                act.at[pl.ds(t * ch, ch), pl.ds(b * BLK, BLK)], gath[t].at[mp * per + b], lsem.at[t, b])
            c.start()
            loc_a.append(c)
    loc_g = []
    for q in range(cols):
        c = pltpu.make_async_copy(grad.at[:, pl.ds(q * BLK, BLK)], gbuf.at[q], gsem.at[q])
        c.start()
        loc_g.append(c)

    barrier = pltpu.get_barrier_semaphore()
    peers = [right, left, across, twin, up, down]
    peers += [dev(x, y, rem(zl + d, NZL), zh, core) for d in range(1, NZL)]
    for p in peers:
        pl.semaphore_signal(barrier, inc=1, device_id=p, device_id_type=MESH)
    pl.semaphore_wait(barrier, len(peers))

    sends = []
    names = {}

    def sem_of(name):
        return names.setdefault(name, len(names))

    def send(name, src, dst, to):
        i = sem_of(name)
        c = pltpu.make_async_remote_copy(
            src_ref=src, dst_ref=dst, send_sem=ssem.at[i], recv_sem=rsem.at[i],
            device_id=to, device_id_type=MESH)
        c.start()
        sends.append(c)

    def arrived(name, dst):
        i = sem_of(name)
        pltpu.make_async_remote_copy(
            src_ref=dst, dst_ref=dst, send_sem=ssem.at[i], recv_sem=rsem.at[i],
            device_id=twin, device_id_type=MESH).wait_recv()

    other = x * 2 + 1 - zh

    def rows(t, h, m):
        return gath[t].at[pl.ds(m * per, per), pl.ds(h * hf, hf)]

    def whole(t, m):
        return gath[t].at[pl.ds(m * per, per)]

    def spread(side, t, m):
        for h in (0, 1):
            for d, to in ((0, right), (1, left)):
                g = h if d == 0 else 1 - h
                send((side, t, d, g), rows(t, g, m), rows(t, g, m), to)

    def pass_on(side, t, z):
        for d, m, to in ((0, xl * 2 + z, right), (1, xr * 2 + z, left)):
            arrived((side, t, d, d), rows(t, d, m))
            send((side, t, d, "on"), rows(t, d, m), rows(t, d, m), to)

    def rest(side, t, z):
        far = rem(x + 2, NX) * 2 + z
        for d, m in ((0, xl * 2 + z), (1, xr * 2 + z)):
            arrived((side, t, d, 1 - d), rows(t, 1 - d, m))
            arrived((side, t, d, "on"), rows(t, d, far))

    def product(t, cr, dy, zp):
        zt = (3 * zp) % 4
        k = (zt * NY + rem(y + dy, NY)) * 2 + rem(core + cr, 2)
        a = gath[t][tl[0, 0, k]]
        g = gbuf[rem(tl[0, 1, k], cols), pl.ds(t * ch, ch)]
        return lax.dot_general(a, g, (((0,), (0,)), ((), ())), preferred_element_type=jnp.float32)

    def group(t, cr, dy):
        for zp in range(4):
            p = product(t, cr, dy, zp)
            acc[cr, dy, zp] = p if t == 0 else acc[cr, dy, zp] + p

    def multiply(t):
        @pl.loop(0, 16)
        def _(i):
            group(t, div(i, 8), rem(i, 8))

    for c in loc_a:
        c.wait()
    for t in range(T):
        send(("z", t), whole(t, mp), whole(t, mp), across)
    for t in range(T):
        spread("own", t, mp)
    for c in loc_g:
        c.wait()
    for t in range(T):
        pass_on("own", t, zh)
        arrived(("z", t), whole(t, other))
        spread("par", t, other)
        if t >= 1:
            pass_on("par", t - 1, 1 - zh)
        if t >= 2:
            rest("own", t - 2, zh)
            rest("par", t - 2, 1 - zh)
            multiply(t - 2)
    pass_on("par", T - 1, 1 - zh)
    for t in (T - 2, T - 1):
        rest("own", t, zh)
        rest("par", t, 1 - zh)
        if t < T - 1:
            multiply(t)

    lo, hi = pl.ds(0, 2), pl.ds(2, 2)

    def last(dy):
        group(T - 1, 1, dy)
        send(("core", dy), acc.at[1, dy], crecv.at[dy], twin)
        group(T - 1, 0, dy)

    def ready(dy):
        arrived(("core", dy), crecv.at[dy])
        acc[0, dy] = acc[0, dy] + crecv[dy]

    def step(plus, dist, half, add):
        buf, to = (yrp, up) if plus else (yrm, down)
        dy = dist if plus else (NY - dist) % NY
        part = lo if half == 0 else hi
        if add:
            arrived(("y", plus, dist, half), buf.at[dist, part])
            acc[0, dy, part] = acc[0, dy, part] + buf[dist, part]
        if dist:
            send(("y", plus, dist - 1, half), acc.at[0, dy, part], buf.at[dist - 1, part], to)

    last(4)
    last(3)
    ready(4)
    step(True, 4, 1, False)
    step(False, 4, 0, False)
    last(5)
    ready(3)
    step(True, 3, 0, False)
    last(2)
    ready(5)
    step(False, 3, 1, False)
    last(6)
    step(True, 3, 1, True)
    step(False, 3, 0, True)
    ready(2)
    step(True, 2, 0, True)
    last(1)
    ready(6)
    step(False, 2, 1, True)
    last(7)
    step(True, 2, 1, True)
    step(False, 2, 0, True)
    ready(1)
    step(True, 1, 0, True)
    last(0)
    ready(7)
    step(False, 1, 1, True)
    step(True, 1, 1, True)
    step(False, 1, 0, True)
    ready(0)

    zsends = []
    zbase = len(names)
    for half in (0, 1):
        step(True, 0, half, True)
        step(False, 0, half, True)
        for zp in (2 * half, 2 * half + 1):
            zt = (3 * zp) % 4
            slot = rem(zl - zt + NZL, NZL)
            c = pltpu.make_async_remote_copy(
                src_ref=acc.at[0, 0, zp], dst_ref=zrecv.at[slot], send_sem=ssem.at[zbase + zp],
                recv_sem=rsem.at[zbase + slot], device_id=dev(x, y, zt, zh, core), device_id_type=MESH)
            pl.when(zl != zt)(c.start)
            zsends.append((zt, c))
    total = acc[0, 0, rem(3 * zl, 4)]
    for slot in range(1, NZL):
        pltpu.make_async_remote_copy(
            src_ref=zrecv.at[slot], dst_ref=zrecv.at[slot], send_sem=ssem.at[zbase],
            recv_sem=rsem.at[zbase + slot], device_id=twin, device_id_type=MESH).wait_recv()
        total = total + zrecv[slot]
    out[0, 0] = total

    for c in sends:
        c.wait_send()
    for zt, c in zsends:
        pl.when(zl != zt)(c.wait_send)
    assert zbase + NZL <= 100


def on_device(activations, out_grad, tile_list, tile_count):
    tokens, feats = activations.shape
    n_mp = NX * 2
    ch = tokens // T
    tile = (BLK, BLK)
    tiles = pl.pallas_call(
        kernel,
        out_shape=jax.ShapeDtypeStruct((1, 1, *tile), jnp.float32),
        in_specs=[
            pl.BlockSpec(memory_space=pltpu.SMEM),
            pl.BlockSpec(memory_space=pl.ANY),
            pl.BlockSpec(memory_space=pl.ANY),
        ],
        out_specs=pl.BlockSpec(memory_space=pltpu.VMEM),
        scratch_shapes=[pltpu.VMEM((n_mp * feats // BLK, ch, BLK), jnp.bfloat16) for _ in range(T)]
        + [
            pltpu.VMEM((out_grad.shape[1] // BLK, tokens, BLK), jnp.bfloat16),
            pltpu.VMEM((2, NY, NZL, *tile), jnp.float32),
            pltpu.VMEM((NY, NZL, *tile), jnp.float32),
            pltpu.VMEM((4, NZL, *tile), jnp.float32),
            pltpu.VMEM((4, NZL, *tile), jnp.float32),
            pltpu.VMEM((NZL, *tile), jnp.float32),
            pltpu.SemaphoreType.DMA((T, feats // BLK)),
            pltpu.SemaphoreType.DMA((out_grad.shape[1] // BLK,)),
            pltpu.SemaphoreType.DMA((100,)),
            pltpu.SemaphoreType.DMA((100,)),
        ],
        compiler_params=pltpu.CompilerParams(
            collective_id=0, has_side_effects=True, vmem_limit_bytes=62 * 1024 * 1024
        ),
    )(jnp.swapaxes(tile_list, 1, 2), activations, out_grad)
    return jnp.where(lax.axis_index("dp") < tile_count[0], tiles, 0.0)


def solution(mesh):
    placed = (P("dp", "mp"), P("dp", "mp"), P("mp", None, None), P("mp"))
    return jax.shard_map(
        on_device, mesh=mesh, in_specs=placed, out_specs=P("mp", "dp", None, None), check_vma=False
    )
```

time: 575 us -> 126 us (0.22)
  the two profiles are of different devices: /device:TPU:2 before, /device:TPU:24 now
where the time goes in v1:
time: 126 us
  Pallas kernels  124 us (98%)
  other arithmetic  1.49 us (1%)
    pallas_call x1, Pallas kernels, on_device(): pl.pallas_call(kernel, out_shape=jax.ShapeDtypeStruct((1, 1, *tile), jnp....  124 us

profile of v1, /device:TPU:24, one launch (start us, length us, event | category | flops | bytes accessed | tf_op | source)
XLA Modules:
  0.0 126.2 jit_solution(780361103892272139)
XLA Ops:
  0.7 124.1 %shard_map.46 = f32[1,1,128,128]{3,2,1,0:T(8,128)} custom-call(s32[1,2,64]{2,1,0:T(2,128)} %bitcast.3, bf16[1024,512]{1,0:T(8,128)(2,1)} %act.1, bf16[1024,1792]{1,0:T(8,128)(2,1)} %grad.1), custom_call_target="tpu_custom_call" | custom-call | tf_op jit(solution)/shard_map/pallas_call | solution.py:236
  124.7 1.5 %broadcast_select_fusion = f32[1,1,128,128]{3,2,1,0:T(8,128)} fusion(f32[1,1,128,128]{3,2,1,0:T(8,128)} %shard_map.46, pred[]{:T(512)S(6)} %lt.3), kind=kLoop, calls=%fused_computation | loop fusion | flops 16384 | bytes 131073 | tf_op jit(solution)/shard_map/jit(_where)/select_n | solution.py:262

commit v2 on v1

--- a/solution.py
+++ b/solution.py
@@ -11,6 +11,34 @@
 T = 4
 
 
+RANGE = 32000.0
+CODE = BLK + 8
+
+
+def encode(tiles):
+    codes, exps = [], []
+    for v in tiles:
+        rows = v.reshape(BLK // 8, 8, BLK)
+        peak = jnp.max(jnp.abs(rows), axis=0)
+        e = jnp.ceil(jnp.log2(jnp.maximum(peak, 1e-30)))
+        q = jnp.round(rows * (RANGE * jnp.exp2(-e))[None])
+        codes.append(q.reshape(BLK, BLK))
+        exps.append(e)
+    if len(exps) == 1:
+        exps = exps * 2
+    return jnp.concatenate(codes + exps, axis=0).astype(jnp.int32).astype(jnp.int16)
+
+
+def decode(code, n):
+    v = code.astype(jnp.int32).astype(jnp.float32)
+    out = []
+    for i in range(n):
+        e = v[n * BLK + 8 * i : n * BLK + 8 * i + 8]
+        rows = v[i * BLK : (i + 1) * BLK].reshape(BLK // 8, 8, BLK)
+        out.append((rows * (jnp.exp2(e) * (1.0 / RANGE))[None]).reshape(BLK, BLK))
+    return out
+
+
 def rem(a, b):
     return lax.rem(a, jnp.int32(b))
 
@@ -21,7 +49,7 @@
 
 def kernel(tl, act, grad, out, *scratch):
     gath = scratch[:T]
-    gbuf, acc, crecv, yrp, yrm, zrecv, lsem, gsem, ssem, rsem = scratch[T:]
+    gbuf, acc, csend, crecv, ysend, yrecv, zsend, zrecv, lsem, gsem, ssem, rsem = scratch[T:]
     tokens, feats = act.shape
     ch = tokens // T
     hf = ch // 2
@@ -40,6 +68,12 @@
     across = dev(x, y, zl, 1 - zh, core)
     twin = dev(x, y, zl, zh, 1 - core)
     up, down = dev(x, rem(y + 1, NY), zl, zh, core), dev(x, rem(y + NY - 1, NY), zl, zh, core)
+
+    barrier = pltpu.get_barrier_semaphore()
+    peers = [right, left, across, twin, up, down]
+    peers += [dev(x, y, rem(zl + d, NZL), zh, core) for d in range(1, NZL)]
+    for p in peers:
+        pl.semaphore_signal(barrier, inc=1, device_id=p, device_id_type=MESH)
 
     loc_a = []
     for t in range(T):
@@ -54,11 +88,6 @@
         c.start()
         loc_g.append(c)
 
-    barrier = pltpu.get_barrier_semaphore()
-    peers = [right, left, across, twin, up, down]
-    peers += [dev(x, y, rem(zl + d, NZL), zh, core) for d in range(1, NZL)]
-    for p in peers:
-        pl.semaphore_signal(barrier, inc=1, device_id=p, device_id_type=MESH)
     pl.semaphore_wait(barrier, len(peers))
 
     sends = []
@@ -148,26 +177,31 @@
         if t < T - 1:
             multiply(t)
 
-    lo, hi = pl.ds(0, 2), pl.ds(2, 2)
-
     def last(dy):
         group(T - 1, 1, dy)
-        send(("core", dy), acc.at[1, dy], crecv.at[dy], twin)
+        for h in (0, 1):
+            csend[dy, h] = encode([acc[1, dy, 2 * h], acc[1, dy, 2 * h + 1]])
+        send(("core", dy), csend.at[dy], crecv.at[dy], twin)
         group(T - 1, 0, dy)
+
+    def add(dy, half, code):
+        for zp, v in zip((2 * half, 2 * half + 1), decode(code, 2)):
+            acc[0, dy, zp] = acc[0, dy, zp] + v
 
     def ready(dy):
         arrived(("core", dy), crecv.at[dy])
-        acc[0, dy] = acc[0, dy] + crecv[dy]
-
-    def step(plus, dist, half, add):
-        buf, to = (yrp, up) if plus else (yrm, down)
+        for h in (0, 1):
+            add(dy, h, crecv[dy, h])
+
+    def step(plus, dist, half, join):
+        way, to = (0, up) if plus else (1, down)
         dy = dist if plus else (NY - dist) % NY
-        part = lo if half == 0 else hi
-        if add:
-            arrived(("y", plus, dist, half), buf.at[dist, part])
-            acc[0, dy, part] = acc[0, dy, part] + buf[dist, part]
+        if join:
+            arrived(("y", plus, dist, half), yrecv.at[way, dist, half])
+            add(dy, half, yrecv[way, dist, half])
         if dist:
-            send(("y", plus, dist - 1, half), acc.at[0, dy, part], buf.at[dist - 1, part], to)
+            ysend[way, dist - 1, half] = encode([acc[0, dy, 2 * half], acc[0, dy, 2 * half + 1]])
+            send(("y", plus, dist - 1, half), ysend.at[way, dist - 1, half], yrecv.at[way, dist - 1, half], to)
 
     last(4)
     last(3)
@@ -208,8 +242,9 @@
         for zp in (2 * half, 2 * half + 1):
             zt = (3 * zp) % 4
             slot = rem(zl - zt + NZL, NZL)
+            zsend[zp] = encode([acc[0, 0, zp]])
             c = pltpu.make_async_remote_copy(
-                src_ref=acc.at[0, 0, zp], dst_ref=zrecv.at[slot], send_sem=ssem.at[zbase + zp],
+                src_ref=zsend.at[zp], dst_ref=zrecv.at[slot], send_sem=ssem.at[zbase + zp],
                 recv_sem=rsem.at[zbase + slot], device_id=dev(x, y, zt, zh, core), device_id_type=MESH)
             pl.when(zl != zt)(c.start)
             zsends.append((zt, c))
@@ -218,7 +253,7 @@
         pltpu.make_async_remote_copy(
             src_ref=zrecv.at[slot], dst_ref=zrecv.at[slot], send_sem=ssem.at[zbase],
             recv_sem=rsem.at[zbase + slot], device_id=twin, device_id_type=MESH).wait_recv()
-        total = total + zrecv[slot]
+        total = total + decode(zrecv[slot], 1)[0]
     out[0, 0] = total
 
     for c in sends:
@@ -246,10 +281,12 @@
         + [
             pltpu.VMEM((out_grad.shape[1] // BLK, tokens, BLK), jnp.bfloat16),
             pltpu.VMEM((2, NY, NZL, *tile), jnp.float32),
-            pltpu.VMEM((NY, NZL, *tile), jnp.float32),
-            pltpu.VMEM((4, NZL, *tile), jnp.float32),
-            pltpu.VMEM((4, NZL, *tile), jnp.float32),
-            pltpu.VMEM((NZL, *tile), jnp.float32),
+            pltpu.VMEM((NY, 2, 2 * CODE, BLK), jnp.int16),
+            pltpu.VMEM((NY, 2, 2 * CODE, BLK), jnp.int16),
+            pltpu.VMEM((2, 4, 2, 2 * CODE, BLK), jnp.int16),
+            pltpu.VMEM((2, 4, 2, 2 * CODE, BLK), jnp.int16),
+            pltpu.VMEM((NZL, BLK + 16, BLK), jnp.int16),
+            pltpu.VMEM((NZL, BLK + 16, BLK), jnp.int16),
             pltpu.SemaphoreType.DMA((T, feats // BLK)),
             pltpu.SemaphoreType.DMA((out_grad.shape[1] // BLK,)),
             pltpu.SemaphoreType.DMA((100,)),

time: 126 us -> 117 us (0.929)
  the two profiles are of different devices: /device:TPU:24 before, /device:TPU:8 now
where the time goes in v2:
time: 117 us
  Pallas kernels  115 us (98%)
  other arithmetic  1.49 us (1%)
    pallas_call x1, Pallas kernels, on_device(): pl.pallas_call(kernel, out_shape=jax.ShapeDtypeStruct((1, 1, *tile), jnp....  115 us

profile of v2, /device:TPU:8, one launch (start us, length us, event | category | flops | bytes accessed | tf_op | source)
XLA Modules:
  0.0 117.2 jit_solution(16440773100566082562)
XLA Ops:
  0.7 115.0 %shard_map.46 = f32[1,1,128,128]{3,2,1,0:T(8,128)} custom-call(s32[1,2,64]{2,1,0:T(2,128)} %bitcast.3, bf16[1024,512]{1,0:T(8,128)(2,1)} %act.1, bf16[1024,1792]{1,0:T(8,128)(2,1)} %grad.1), custom_call_target="tpu_custom_call" | custom-call | tf_op jit(solution)/shard_map/pallas_call | solution.py:271
  115.7 1.5 %broadcast_select_fusion = f32[1,1,128,128]{3,2,1,0:T(8,128)} fusion(f32[1,1,128,128]{3,2,1,0:T(8,128)} %shard_map.46, pred[]{:T(512)S(6)} %lt.3), kind=kLoop, calls=%fused_computation | loop fusion | flops 16384 | bytes 131073 | tf_op jit(solution)/shard_map/jit(_where)/select_n | solution.py:299

commit v3 on v0

v3 whole, which is shorter than its diff:
```python
import jax
import jax.numpy as jnp
from jax import lax
from jax.experimental import pallas as pl
from jax.experimental.pallas import tpu as pltpu
from jax.sharding import PartitionSpec as P

MESH = pl.DeviceIdType.MESH
BLK = 128
NX, NY, NZL = 4, 8, 4
T = 4
NSEM = 65


RANGE = 32000.0
CODE = BLK + 16


def encode(v):
    rows = v.reshape(BLK // 16, 16, BLK)
    peak = jnp.max(jnp.abs(rows), axis=0)
    e = jnp.ceil(jnp.log2(jnp.maximum(peak, 1e-30)))
    q = jnp.round(rows * (RANGE * jnp.exp2(-e))[None])
    return jnp.concatenate([q.reshape(BLK, BLK), e], axis=0).astype(jnp.int32).astype(jnp.int16)


def decode(code):
    v = code.astype(jnp.int32).astype(jnp.float32)
    scale = jnp.exp2(v[BLK:]) * (1.0 / RANGE)
    return (v[:BLK].reshape(BLK // 16, 16, BLK) * scale[None]).reshape(BLK, BLK)


def rem(a, b):
    return lax.rem(a, jnp.int32(b))


def div(a, b):
    return lax.div(a, jnp.int32(b))


def kernel(tl, act, grad, out, *scratch):
    gath = scratch[:T]
    araw, gbuf, acc, csend, crecv, ysend, yrecv, zsend, zrecv, lsem, ssem, rsem = scratch[T:]
    tokens, feats = act.shape
    ch = tokens // T
    hf = ch // 2
    cols = grad.shape[1] // BLK
    per = feats // BLK

    dp, mp = lax.axis_index("dp"), lax.axis_index("mp")
    core, y, zl = rem(dp, 2), rem(div(dp, 2), NY), div(dp, 2 * NY)
    x, zh = div(mp, 2), rem(mp, 2)

    def dev(x_, y_, zl_, zh_, core_):
        return ((zl_ * NY + y_) * 2 + core_, x_ * 2 + zh_)

    xr, xl = rem(x + 1, NX), rem(x + NX - 1, NX)
    right, left = dev(xr, y, zl, zh, core), dev(xl, y, zl, zh, core)
    across = dev(x, y, zl, 1 - zh, core)
    twin = dev(x, y, zl, zh, 1 - core)
    up, down = dev(x, rem(y + 1, NY), zl, zh, core), dev(x, rem(y + NY - 1, NY), zl, zh, core)

    barrier = pltpu.get_barrier_semaphore()
    peers = [across, right, left, twin, up, down]
    peers += [dev(x, y, rem(zl + d, NZL), zh, core) for d in range(1, NZL)]
    for p in peers:
        pl.semaphore_signal(barrier, inc=1, device_id=p, device_id_type=MESH)

    loc = []
    for t in range(T):
        c = pltpu.make_async_copy(act.at[pl.ds(t * ch, ch)], araw.at[pl.ds(t * ch, ch)], lsem.at[t])
        c.start()
        loc.append(c)
    for q in range(cols):
        pltpu.make_async_copy(grad.at[:, pl.ds(q * BLK, BLK)], gbuf.at[q], lsem.at[T]).start()
    for t in range(T):
        loc[t].wait()
        for h in (0, 1):
            for b in range(per):
                part = araw[t * ch + h * hf : t * ch + (h + 1) * hf, b * BLK : (b + 1) * BLK]
                gath[t][mp * per + b, h] = part.T
    pl.semaphore_wait(barrier, len(peers))

    names = {}

    def send(group, name, src, dst, to):
        i = names.setdefault(name, len(names))
        pltpu.make_async_remote_copy(
            src_ref=src, dst_ref=dst, send_sem=ssem.at[group], recv_sem=rsem.at[i],
            device_id=to, device_id_type=MESH).start()

    def arrived(name, dst):
        i = names.setdefault(name, len(names))
        pltpu.make_async_remote_copy(
            src_ref=dst, dst_ref=dst, send_sem=ssem.at[0], recv_sem=rsem.at[i],
            device_id=twin, device_id_type=MESH).wait_recv()

    def sent(group, ref):
        pltpu.make_async_remote_copy(
            src_ref=ref, dst_ref=ref, send_sem=ssem.at[group], recv_sem=rsem.at[0],
            device_id=twin, device_id_type=MESH).wait_send()

    def rows(t, h, m):
        return gath[t].at[pl.ds(m * per, per), h]

    def whole(t, m):
        return gath[t].at[pl.ds(m * per, per)]

    def spread(side, t, m):
        for h in (0, 1):
            for d, to in ((0, right), (1, left)):
                g = h if d == 0 else 1 - h
                name = (side, t, d) if h == 0 else (side, t)
                send(t, name, rows(t, g, m), rows(t, g, m), to)

    def pass_on(side, t):
        z = zh if side == "own" else 1 - zh
        for d, m, to in ((0, xl * 2 + z, right), (1, xr * 2 + z, left)):
            arrived((side, t, d), rows(t, d, m))
            send(t, (side, t), rows(t, d, m), rows(t, d, m), to)

    def rest(t):
        for side in ("own", "par"):
            arrived((side, t), gath[t].at[pl.ds(0, 2 * per)])

    def cross(t):
        m = x * 2 + 1 - zh
        arrived(("z", t), whole(t, m))
        spread("par", t, m)

    def group(t, cr, dy):
        for zp in range(NZL):
            zt = (3 * zp) % NZL
            k = (zt * NY + rem(y + dy, NY)) * 2 + rem(core + cr, 2)
            a = gath[t][tl[0, 0, k]]
            g = gbuf[rem(tl[0, 1, k], cols), pl.ds(t * ch, ch)]
            p = jnp.dot(jnp.concatenate([a[0], a[1]], axis=1), g, preferred_element_type=jnp.float32)
            acc[cr, dy, zp] = p if t == 0 else acc[cr, dy, zp] + p

    def multiply(t):
        @pl.loop(0, 2 * NY)
        def _(i):
            group(t, div(i, NY), rem(i, NY))

    for t in range(T):
        send(t, ("z", t), whole(t, mp), whole(t, mp), across)
    for t in range(T):
        spread("own", t, mp)
    for t in range(T):
        pass_on("own", t)
    pltpu.make_async_copy(gbuf, gbuf, lsem.at[T]).wait()
    cross(0)
    cross(1)
    pass_on("par", 0)
    cross(2)
    pass_on("par", 1)
    rest(0)
    multiply(0)
    pass_on("par", 2)
    cross(3)
    rest(1)
    multiply(1)
    pass_on("par", 3)
    rest(2)
    multiply(2)
    rest(3)

    def last(dy):
        group(T - 1, 1, dy)
        for zp in range(NZL):
            csend[dy, zp] = encode(acc[1, dy, zp])
        send(T, ("core", dy), csend.at[dy], crecv.at[dy], twin)
        group(T - 1, 0, dy)

    def ready(dy):
        arrived(("core", dy), crecv.at[dy])
        for zp in range(NZL):
            acc[0, dy, zp] = acc[0, dy, zp] + decode(crecv[dy, zp])

    def step(way, dist, zp):
        dy = dist if way == 0 else (NY - dist) % NY
        long = (zp >= 2) == (way == 0)
        v = acc[0, dy, zp]
        if dist < (4 if long else 3):
            arrived(("y", way, dist, zp), yrecv.at[way, dist, zp])
            v = v + decode(yrecv[way, dist, zp])
        ysend[way, (4 - dist) * NZL + (zp + 2 * (1 - way)) % NZL] = encode(v)
        send(
            T + 1 + way, ("y", way, dist - 1, zp),
            ysend.at[way, (4 - dist) * NZL + (zp + 2 * (1 - way)) % NZL],
            yrecv.at[way, dist - 1, zp], (up, down)[way])

    def steps(dist, part):
        for i in (0, 1):
            for way in (0, 1):
                step(way, dist, 2 * (part if way == 0 else 1 - part) + i)

    last(4)
    last(3)
    ready(4)
    steps(4, 1)
    last(5)
    ready(3)
    ready(5)
    steps(3, 0)
    last(2)
    last(6)
    steps(3, 1)
    ready(2)
    ready(6)
    steps(2, 0)
    last(1)
    last(7)
    steps(2, 1)
    ready(1)
    ready(7)
    steps(1, 0)
    last(0)
    steps(1, 1)
    ready(0)

    zs = T + 3
    for part in (0, 1):
        for zp in (2 * part, 2 * part + 1):
            v = acc[0, 0, zp]
            for way in (0, 1):
                arrived(("y", way, 0, zp), yrecv.at[way, 0, zp])
                v = v + decode(yrecv[way, 0, zp])
            acc[0, 0, zp] = v
            zt = (3 * zp) % NZL
            slot = rem(zl - zt + NZL, NZL)
            zsend[zp] = encode(v)
            i = names.setdefault("line", len(names))
            c = pltpu.make_async_remote_copy(
                src_ref=zsend.at[zp], dst_ref=zrecv.at[slot], send_sem=ssem.at[zs],
                recv_sem=rsem.at[i], device_id=dev(x, y, zt, zh, core), device_id_type=MESH)
            pl.when(zl != zt)(c.start)
    total = acc[0, 0, rem(3 * zl, NZL)]
    arrived("line", zrecv.at[pl.ds(1, NZL - 1)])
    for slot in range(1, NZL):
        total = total + decode(zrecv[slot])
    out[0, 0] = total

    for t in range(T):
        sent(t, gath[t].at[pl.ds(0, 7 * per)])
    sent(T, csend)
    for way in (0, 1):
        sent(T + 1 + way, ysend.at[way, pl.ds(2, 4 * NZL - 2)])
    sent(zs, zsend.at[pl.ds(1, NZL - 1)])
    assert len(names) <= NSEM


def on_device(activations, out_grad, tile_list, tile_count):
    tokens, feats = activations.shape
    n_mp = NX * 2
    ch = tokens // T
    tiles = pl.pallas_call(
        kernel,
        out_shape=jax.ShapeDtypeStruct((1, 1, BLK, BLK), jnp.float32),
        in_specs=[
            pl.BlockSpec(memory_space=pltpu.SMEM),
            pl.BlockSpec(memory_space=pl.ANY),
            pl.BlockSpec(memory_space=pl.ANY),
        ],
        out_specs=pl.BlockSpec(memory_space=pltpu.VMEM),
        scratch_shapes=[
            pltpu.VMEM((n_mp * feats // BLK, 2, BLK, ch // 2), jnp.bfloat16) for _ in range(T)
        ]
        + [
            pltpu.VMEM(activations.shape, jnp.bfloat16),
            pltpu.VMEM((out_grad.shape[1] // BLK, tokens, BLK), jnp.bfloat16),
            pltpu.VMEM((2, NY, NZL, BLK, BLK), jnp.float32),
            pltpu.VMEM((NY, NZL, CODE, BLK), jnp.int16),
            pltpu.VMEM((NY, NZL, CODE, BLK), jnp.int16),
            pltpu.VMEM((2, 4 * NZL, CODE, BLK), jnp.int16),
            pltpu.VMEM((2, 4, NZL, CODE, BLK), jnp.int16),
            pltpu.VMEM((NZL, CODE, BLK), jnp.int16),
            pltpu.VMEM((NZL, CODE, BLK), jnp.int16),
            pltpu.SemaphoreType.DMA((T + 1,)),
            pltpu.SemaphoreType.DMA((T + 4,)),
            pltpu.SemaphoreType.DMA((NSEM,)),
        ],
        compiler_params=pltpu.CompilerParams(
            collective_id=0, has_side_effects=True, vmem_limit_bytes=62 * 1024 * 1024
        ),
    )(jnp.swapaxes(tile_list, 1, 2), activations, out_grad)
    return jnp.where(lax.axis_index("dp") < tile_count[0], tiles, 0.0)


def solution(mesh):
    placed = (P("dp", "mp"), P("dp", "mp"), P("mp", None, None), P("mp"))
    return jax.shard_map(
        on_device, mesh=mesh, in_specs=placed, out_specs=P("mp", "dp", None, None), check_vma=False
    )
```

time: 575 us -> 107 us (0.19)
  the two profiles are of different devices: /device:TPU:2 before, /device:TPU:24 now
where the time goes in v3:
time: 107 us
  Pallas kernels  105 us (98%)
  other arithmetic  1.49 us (1%)
    pallas_call x1, Pallas kernels, on_device(): pl.pallas_call(kernel, out_shape=jax.ShapeDtypeStruct((1, 1, BLK, BLK), j...  105 us

profile of v3, /device:TPU:24, one launch (start us, length us, event | category | flops | bytes accessed | tf_op | source)
XLA Modules:
  0.0 106.9 jit_solution(10247952255133430109)
XLA Ops:
  0.7 104.7 %shard_map.46 = f32[1,1,128,128]{3,2,1,0:T(8,128)} custom-call(s32[1,2,64]{2,1,0:T(2,128)} %bitcast.3, bf16[1024,512]{1,0:T(8,128)(2,1)} %act.1, bf16[1024,1792]{1,0:T(8,128)(2,1)} %grad.1), custom_call_target="tpu_custom_call" | custom-call | tf_op jit(solution)/shard_map/pallas_call | solution.py:257
  105.4 1.5 %broadcast_select_fusion = f32[1,1,128,128]{3,2,1,0:T(8,128)} fusion(f32[1,1,128,128]{3,2,1,0:T(8,128)} %shard_map.46, pred[]{:T(512)S(6)} %lt.3), kind=kLoop, calls=%fused_computation | loop fusion | flops 16384 | bytes 131073 | tf_op jit(solution)/shard_map/jit(_where)/select_n | solution.py:287

commit v4 on v3

--- a/solution.py
+++ b/solution.py
@@ -9,7 +9,7 @@
 BLK = 128
 NX, NY, NZL = 4, 8, 4
 T = 4
-NSEM = 65
+NSEM = 66
 
 
 RANGE = 32000.0
@@ -73,12 +73,15 @@
         loc.append(c)
     for q in range(cols):
         pltpu.make_async_copy(grad.at[:, pl.ds(q * BLK, BLK)], gbuf.at[q], lsem.at[T]).start()
-    for t in range(T):
+
+    def turn(t):
         loc[t].wait()
         for h in (0, 1):
             for b in range(per):
                 part = araw[t * ch + h * hf : t * ch + (h + 1) * hf, b * BLK : (b + 1) * BLK]
                 gath[t][mp * per + b, h] = part.T
+
+    turn(0)
     pl.semaphore_wait(barrier, len(peers))
 
     names = {}
@@ -100,28 +103,32 @@
             src_ref=ref, dst_ref=ref, send_sem=ssem.at[group], recv_sem=rsem.at[0],
             device_id=twin, device_id_type=MESH).wait_send()
 
-    def rows(t, h, m):
-        return gath[t].at[pl.ds(m * per, per), h]
+    mix = T - 1
 
     def whole(t, m):
         return gath[t].at[pl.ds(m * per, per)]
+
+    def part(side, t, d, m):
+        if side == "par" and t == mix:
+            return gath[t].at[pl.ds(m * per + d * (per // 2), per // 2), 0]
+        return gath[t].at[pl.ds(m * per, per), d]
 
     def spread(side, t, m):
         for h in (0, 1):
             for d, to in ((0, right), (1, left)):
                 g = h if d == 0 else 1 - h
                 name = (side, t, d) if h == 0 else (side, t)
-                send(t, name, rows(t, g, m), rows(t, g, m), to)
+                send(t, name, part(side, t, g, m), part(side, t, g, m), to)
 
     def pass_on(side, t):
         z = zh if side == "own" else 1 - zh
         for d, m, to in ((0, xl * 2 + z, right), (1, xr * 2 + z, left)):
-            arrived((side, t, d), rows(t, d, m))
-            send(t, (side, t), rows(t, d, m), rows(t, d, m), to)
-
-    def rest(t):
-        for side in ("own", "par"):
-            arrived((side, t), gath[t].at[pl.ds(0, 2 * per)])
+            arrived((side, t, d), part(side, t, d, m))
+            send(t, (side, t), part(side, t, d, m), part(side, t, d, m), to)
+
+    def rest(side, t):
+        n = per if side == "par" and t == mix else 2 * per
+        arrived((side, t), gath[t].at[pl.ds(0, n)])
 
     def cross(t):
         m = x * 2 + 1 - zh
@@ -138,39 +145,63 @@
             acc[cr, dy, zp] = p if t == 0 else acc[cr, dy, zp] + p
 
     def multiply(t):
-        @pl.loop(0, 2 * NY)
-        def _(i):
-            group(t, div(i, NY), rem(i, NY))
-
-    for t in range(T):
+        @pl.loop(0, NY)
+        def _(dy):
+            group(t, 0, dy)
+            group(t, 1, dy)
+
+    def cross_own(t):
         send(t, ("z", t), whole(t, mp), whole(t, mp), across)
-    for t in range(T):
+
+    cross_own(0)
+    spread("own", 0, mp)
+    for t in range(1, T):
+        turn(t)
         spread("own", t, mp)
-    for t in range(T):
-        pass_on("own", t)
+    pass_on("own", 0)
+    cross_own(1)
+    pass_on("own", 1)
+    pass_on("own", 2)
+    cross_own(2)
+    pass_on("own", 3)
+    cross_own(3)
     pltpu.make_async_copy(gbuf, gbuf, lsem.at[T]).wait()
     cross(0)
     cross(1)
+    rest("own", mix)
+    for x_ in (xl, xr, rem(x + 2, NX)):
+        half = gath[mix].at[pl.ds((x_ * 2 + zh) * per, per), 1]
+        send(mix, "late", half, half, across)
     pass_on("par", 0)
     cross(2)
     pass_on("par", 1)
-    rest(0)
+    rest("own", 0)
+    rest("par", 0)
     multiply(0)
     pass_on("par", 2)
     cross(3)
-    rest(1)
+    rest("own", 1)
+    rest("par", 1)
     multiply(1)
     pass_on("par", 3)
-    rest(2)
+    rest("own", 2)
+    rest("par", 2)
     multiply(2)
-    rest(3)
-
-    def last(dy):
+    rest("par", 3)
+    arrived("late", gath[mix].at[pl.ds(0, 3 * per // 2)])
+
+    def give(dy):
         group(T - 1, 1, dy)
         for zp in range(NZL):
             csend[dy, zp] = encode(acc[1, dy, zp])
         send(T, ("core", dy), csend.at[dy], crecv.at[dy], twin)
+
+    def keep(dy):
         group(T - 1, 0, dy)
+
+    def last(dy):
+        give(dy)
+        keep(dy)
 
     def ready(dy):
         arrived(("core", dy), crecv.at[dy])
@@ -195,11 +226,14 @@
             for way in (0, 1):
                 step(way, dist, 2 * (part if way == 0 else 1 - part) + i)
 
-    last(4)
-    last(3)
+    give(4)
+    give(3)
+    keep(4)
+    give(5)
+    keep(3)
     ready(4)
     steps(4, 1)
-    last(5)
+    keep(5)
     ready(3)
     ready(5)
     steps(3, 0)

time: 107 us -> 106 us (level)
  the two profiles are of different devices: /device:TPU:24 before, /device:TPU:74 now
where the time goes in v4:
time: 106 us
  Pallas kernels  104 us (98%)
  other arithmetic  1.49 us (1%)
    pallas_call x1, Pallas kernels, on_device(): pl.pallas_call(kernel, out_shape=jax.ShapeDtypeStruct((1, 1, BLK, BLK), j...  104 us

profile of v4, /device:TPU:74, one launch (start us, length us, event | category | flops | bytes accessed | tf_op | source)
XLA Modules:
  0.0 105.9 jit_solution(16934358846261500714)
XLA Ops:
  0.7 103.7 %shard_map.46 = f32[1,1,128,128]{3,2,1,0:T(8,128)} custom-call(s32[1,2,64]{2,1,0:T(2,128)} %bitcast.3, bf16[1024,512]{1,0:T(8,128)(2,1)} %act.1, bf16[1024,1792]{1,0:T(8,128)(2,1)} %grad.1), custom_call_target="tpu_custom_call" | custom-call | tf_op jit(solution)/shard_map/pallas_call | solution.py:291
  104.4 1.5 %broadcast_select_fusion = f32[1,1,128,128]{3,2,1,0:T(8,128)} fusion(f32[1,1,128,128]{3,2,1,0:T(8,128)} %shard_map.46, pred[]{:T(512)S(6)} %lt.3), kind=kLoop, calls=%fused_computation | loop fusion | flops 16384 | bytes 131073 | tf_op jit(solution)/shard_map/jit(_where)/select_n | solution.py:321

commit v5 on v4

--- a/solution.py
+++ b/solution.py
@@ -9,7 +9,7 @@
 BLK = 128
 NX, NY, NZL = 4, 8, 4
 T = 4
-NSEM = 66
+NSEM = 81
 
 
 RANGE = 32000.0
@@ -40,7 +40,7 @@
 
 def kernel(tl, act, grad, out, *scratch):
     gath = scratch[:T]
-    araw, gbuf, acc, csend, crecv, ysend, yrecv, zsend, zrecv, lsem, ssem, rsem = scratch[T:]
+    araw, gbuf, acc, csend, crecv, ysend, yrecv, zsend, zrecv, relay, late, lsem, ssem, rsem = scratch[T:]
     tokens, feats = act.shape
     ch = tokens // T
     hf = ch // 2
@@ -56,12 +56,18 @@
 
     xr, xl = rem(x + 1, NX), rem(x + NX - 1, NX)
     right, left = dev(xr, y, zl, zh, core), dev(xl, y, zl, zh, core)
-    across = dev(x, y, zl, 1 - zh, core)
+    zz = zh * NZL + zl
+
+    def on_ring(q):
+        q = rem(q + 2 * NZL, 2 * NZL)
+        return dev(x, y, rem(q, NZL), div(q, NZL), core)
+
+    ahead, behind = on_ring(zz + 1), on_ring(zz - 1)
     twin = dev(x, y, zl, zh, 1 - core)
     up, down = dev(x, rem(y + 1, NY), zl, zh, core), dev(x, rem(y + NY - 1, NY), zl, zh, core)
 
     barrier = pltpu.get_barrier_semaphore()
-    peers = [across, right, left, twin, up, down]
+    peers = [ahead, behind, right, left, twin, up, down]
     peers += [dev(x, y, rem(zl + d, NZL), zh, core) for d in range(1, NZL)]
     for p in peers:
         pl.semaphore_signal(barrier, inc=1, device_id=p, device_id_type=MESH)
@@ -105,9 +111,6 @@
 
     mix = T - 1
 
-    def whole(t, m):
-        return gath[t].at[pl.ds(m * per, per)]
-
     def part(side, t, d, m):
         if side == "par" and t == mix:
             return gath[t].at[pl.ds(m * per + d * (per // 2), per // 2), 0]
@@ -130,10 +133,41 @@
         n = per if side == "par" and t == mix else 2 * per
         arrived((side, t), gath[t].at[pl.ds(0, n)])
 
+    def any_rows(n):
+        return gath[0].at[pl.ds(0, n)]
+
+    def final(way):
+        return 1 - div(rem(zz + (1, 2 * NZL - 1)[way], 2 * NZL), NZL)
+
+    def hop(t, s):
+        if s > 1:
+            arrived(("z", t, s - 1), any_rows(per))
+        for way, to in ((0, ahead), (1, behind)):
+            src = gath[t].at[pl.ds(mp * per, per), way] if s == 1 else relay.at[way, t, s - 2]
+            dst = relay.at[way, t, s - 1] if s < 4 else gath[t].at[pl.ds((x * 2 + final(way)) * per, per), way]
+            send(t if s == 1 else T + 4, ("z", t, s), src, dst, to)
+
+    def late_hop(s):
+        two = per // 2
+        if s > 1:
+            arrived(("late", s - 1), any_rows(3 * two))
+        for way, to in ((0, ahead), (1, behind)):
+            if s in (2, 3):
+                send(T + 5, ("late", s), late.at[way, s - 2], late.at[way, s - 1], to)
+                continue
+            for j, x_ in enumerate((xl, xr, rem(x + 2, NX))):
+                slot = pl.ds(j * two, two)
+                if s == 1:
+                    src = gath[mix].at[pl.ds((x_ * 2 + zh) * per + way * two, two), 1]
+                    dst = late.at[way, 0, slot]
+                else:
+                    src = late.at[way, 2, slot]
+                    dst = gath[mix].at[pl.ds((x_ * 2 + final(way)) * per + way * two, two), 1]
+                send(T + 5, ("late", s), src, dst, to)
+
     def cross(t):
-        m = x * 2 + 1 - zh
-        arrived(("z", t), whole(t, m))
-        spread("par", t, m)
+        arrived(("z", t, 4), any_rows(per))
+        spread("par", t, x * 2 + 1 - zh)
 
     def group(t, cr, dy):
         for zp in range(NZL):
@@ -150,36 +184,48 @@
             group(t, 0, dy)
             group(t, 1, dy)
 
-    def cross_own(t):
-        send(t, ("z", t), whole(t, mp), whole(t, mp), across)
-
-    cross_own(0)
+    hop(0, 1)
     spread("own", 0, mp)
-    for t in range(1, T):
+    turn(1)
+    hop(1, 1)
+    spread("own", 1, mp)
+    for t in range(2, T):
         turn(t)
         spread("own", t, mp)
+    hop(0, 2)
     pass_on("own", 0)
-    cross_own(1)
+    hop(1, 2)
+    hop(0, 3)
     pass_on("own", 1)
+    hop(1, 3)
+    hop(0, 4)
     pass_on("own", 2)
-    cross_own(2)
+    hop(1, 4)
+    hop(2, 1)
+    hop(3, 1)
     pass_on("own", 3)
-    cross_own(3)
     pltpu.make_async_copy(gbuf, gbuf, lsem.at[T]).wait()
     cross(0)
     cross(1)
+    hop(2, 2)
+    hop(3, 2)
+    hop(2, 3)
     rest("own", mix)
-    for x_ in (xl, xr, rem(x + 2, NX)):
-        half = gath[mix].at[pl.ds((x_ * 2 + zh) * per, per), 1]
-        send(mix, "late", half, half, across)
+    late_hop(1)
+    hop(3, 3)
     pass_on("par", 0)
+    hop(2, 4)
+    hop(3, 4)
+    late_hop(2)
     cross(2)
     pass_on("par", 1)
+    late_hop(3)
     rest("own", 0)
     rest("par", 0)
     multiply(0)
     pass_on("par", 2)
     cross(3)
+    late_hop(4)
     rest("own", 1)
     rest("par", 1)
     multiply(1)
@@ -188,7 +234,7 @@
     rest("par", 2)
     multiply(2)
     rest("par", 3)
-    arrived("late", gath[mix].at[pl.ds(0, 3 * per // 2)])
+    arrived(("late", 4), any_rows(3 * per // 2))
 
     def give(dy):
         group(T - 1, 1, dy)
@@ -276,7 +322,9 @@
     out[0, 0] = total
 
     for t in range(T):
-        sent(t, gath[t].at[pl.ds(0, 7 * per)])
+        sent(t, gath[t].at[pl.ds(0, (11 * per) // 2 if t == mix else 7 * per)])
+    sent(T + 4, relay)
+    sent(T + 5, any_rows(6 * per))
     sent(T, csend)
     for way in (0, 1):
         sent(T + 1 + way, ysend.at[way, pl.ds(2, 4 * NZL - 2)])
@@ -310,8 +358,10 @@
             pltpu.VMEM((2, 4, NZL, CODE, BLK), jnp.int16),
             pltpu.VMEM((NZL, CODE, BLK), jnp.int16),
             pltpu.VMEM((NZL, CODE, BLK), jnp.int16),
+            pltpu.VMEM((2, T, 3, feats // BLK, BLK, ch // 2), jnp.bfloat16),
+            pltpu.VMEM((2, 3, 3 * feats // BLK // 2, BLK, ch // 2), jnp.bfloat16),
             pltpu.SemaphoreType.DMA((T + 1,)),
-            pltpu.SemaphoreType.DMA((T + 4,)),
+            pltpu.SemaphoreType.DMA((T + 6,)),
             pltpu.SemaphoreType.DMA((NSEM,)),
         ],
         compiler_params=pltpu.CompilerParams(

time: 106 us -> 105 us (level)
  the two profiles are of different devices: /device:TPU:74 before, /device:TPU:8 now
where the time goes in v5:
time: 105 us
  Pallas kernels  103 us (98%)
  other arithmetic  1.49 us (1%)
    pallas_call x1, Pallas kernels, on_device(): pl.pallas_call(kernel, out_shape=jax.ShapeDtypeStruct((1, 1, BLK, BLK), j...  103 us

profile of v5, /device:TPU:8, one launch (start us, length us, event | category | flops | bytes accessed | tf_op | source)
XLA Modules:
  0.0 104.9 jit_solution(3931302418341823042)
XLA Ops:
  0.7 102.7 %shard_map.46 = f32[1,1,128,128]{3,2,1,0:T(8,128)} custom-call(s32[1,2,64]{2,1,0:T(2,128)} %bitcast.3, bf16[1024,512]{1,0:T(8,128)(2,1)} %act.1, bf16[1024,1792]{1,0:T(8,128)(2,1)} %grad.1), custom_call_target="tpu_custom_call" | custom-call | tf_op jit(solution)/shard_map/pallas_call | solution.py:339
  103.4 1.5 %broadcast_select_fusion = f32[1,1,128,128]{3,2,1,0:T(8,128)} fusion(f32[1,1,128,128]{3,2,1,0:T(8,128)} %shard_map.46, pred[]{:T(512)S(6)} %lt.3), kind=kLoop, calls=%fused_computation | loop fusion | flops 16384 | bytes 131073 | tf_op jit(solution)/shard_map/jit(_where)/select_n | solution.py:371

commit v6 on v5

--- a/solution.py
+++ b/solution.py
@@ -38,9 +38,9 @@
     return lax.div(a, jnp.int32(b))
 
 
-def kernel(tl, act, grad, out, *scratch):
+def kernel(tiles, act, grad, out, *scratch):
     gath = scratch[:T]
-    araw, gbuf, acc, csend, crecv, ysend, yrecv, zsend, zrecv, relay, late, lsem, ssem, rsem = scratch[T:]
+    araw, gbuf, acc, csend, crecv, ysend, yrecv, zsend, zrecv, relay, late, tl, lsem, ssem, rsem = scratch[T:]
     tokens, feats = act.shape
     ch = tokens // T
     hf = ch // 2
@@ -66,19 +66,21 @@
     twin = dev(x, y, zl, zh, 1 - core)
     up, down = dev(x, rem(y + 1, NY), zl, zh, core), dev(x, rem(y + NY - 1, NY), zl, zh, core)
 
+    loc = []
+    for t in range(T):
+        c = pltpu.make_async_copy(act.at[pl.ds(t * ch, ch)], araw.at[pl.ds(t * ch, ch)], lsem.at[t])
+        c.start()
+        loc.append(c)
+    loc_tl = pltpu.make_async_copy(tiles, tl, lsem.at[T + 1])
+    loc_tl.start()
+    for q in range(cols):
+        pltpu.make_async_copy(grad.at[:, pl.ds(q * BLK, BLK)], gbuf.at[q], lsem.at[T]).start()
+
     barrier = pltpu.get_barrier_semaphore()
     peers = [ahead, behind, right, left, twin, up, down]
     peers += [dev(x, y, rem(zl + d, NZL), zh, core) for d in range(1, NZL)]
     for p in peers:
         pl.semaphore_signal(barrier, inc=1, device_id=p, device_id_type=MESH)
-
-    loc = []
-    for t in range(T):
-        c = pltpu.make_async_copy(act.at[pl.ds(t * ch, ch)], araw.at[pl.ds(t * ch, ch)], lsem.at[t])
-        c.start()
-        loc.append(c)
-    for q in range(cols):
-        pltpu.make_async_copy(grad.at[:, pl.ds(q * BLK, BLK)], gbuf.at[q], lsem.at[T]).start()
 
     def turn(t):
         loc[t].wait()
@@ -205,14 +207,15 @@
     hop(3, 1)
     pass_on("own", 3)
     pltpu.make_async_copy(gbuf, gbuf, lsem.at[T]).wait()
+    loc_tl.wait()
     cross(0)
     cross(1)
     hop(2, 2)
     hop(3, 2)
     hop(2, 3)
     rest("own", mix)
+    hop(3, 3)
     late_hop(1)
-    hop(3, 3)
     pass_on("par", 0)
     hop(2, 4)
     hop(3, 4)
@@ -336,11 +339,12 @@
     tokens, feats = activations.shape
     n_mp = NX * 2
     ch = tokens // T
+    n_slots = tile_list.shape[1]
     tiles = pl.pallas_call(
         kernel,
         out_shape=jax.ShapeDtypeStruct((1, 1, BLK, BLK), jnp.float32),
         in_specs=[
-            pl.BlockSpec(memory_space=pltpu.SMEM),
+            pl.BlockSpec(memory_space=pl.ANY),
             pl.BlockSpec(memory_space=pl.ANY),
             pl.BlockSpec(memory_space=pl.ANY),
         ],
@@ -360,7 +364,8 @@
             pltpu.VMEM((NZL, CODE, BLK), jnp.int16),
             pltpu.VMEM((2, T, 3, feats // BLK, BLK, ch // 2), jnp.bfloat16),
             pltpu.VMEM((2, 3, 3 * feats // BLK // 2, BLK, ch // 2), jnp.bfloat16),
-            pltpu.SemaphoreType.DMA((T + 1,)),
+            pltpu.SMEM((1, 2, n_slots), jnp.int32),
+            pltpu.SemaphoreType.DMA((T + 2,)),
             pltpu.SemaphoreType.DMA((T + 6,)),
             pltpu.SemaphoreType.DMA((NSEM,)),
         ],

time: 105 us -> 104 us (level)
    pallas_call x1, Pallas kernels: 103 us -> 102 us  [on_device(): pl.pallas_call(kernel, out_shape=jax.ShapeDtypeStruct((1, 1, BLK, BLK), j...]
where the time goes in v6:
time: 104 us
  Pallas kernels  102 us (98%)
  other arithmetic  1.49 us (1%)
    pallas_call x1, Pallas kernels, on_device(): pl.pallas_call(kernel, out_shape=jax.ShapeDtypeStruct((1, 1, BLK, BLK), j...  102 us

profile of v6, /device:TPU:8, one launch (start us, length us, event | category | flops | bytes accessed | tf_op | source)
XLA Modules:
  0.0 103.7 jit_solution(3464698155284491592)
XLA Ops:
  0.7 101.5 %shard_map.46 = f32[1,1,128,128]{3,2,1,0:T(8,128)} custom-call(s32[1,2,64]{2,1,0:T(2,128)} %bitcast.3, bf16[1024,512]{1,0:T(8,128)(2,1)} %act.1, bf16[1024,1792]{1,0:T(8,128)(2,1)} %grad.1), custom_call_target="tpu_custom_call" | custom-call | tf_op jit(solution)/shard_map/pallas_call | solution.py:343
  102.2 1.5 %broadcast_select_fusion = f32[1,1,128,128]{3,2,1,0:T(8,128)} fusion(f32[1,1,128,128]{3,2,1,0:T(8,128)} %shard_map.46, pred[]{:T(512)S(6)} %lt.3), kind=kLoop, calls=%fused_computation | loop fusion | flops 16384 | bytes 131073 | tf_op jit(solution)/shard_map/jit(_where)/select_n | solution.py:376

commit v7 on v6

--- a/solution.py
+++ b/solution.py
@@ -222,17 +222,17 @@
     late_hop(2)
     cross(2)
     pass_on("par", 1)
+    cross(3)
+    pass_on("par", 2)
     late_hop(3)
     rest("own", 0)
     rest("par", 0)
     multiply(0)
-    pass_on("par", 2)
-    cross(3)
+    pass_on("par", 3)
     late_hop(4)
     rest("own", 1)
     rest("par", 1)
     multiply(1)
-    pass_on("par", 3)
     rest("own", 2)
     rest("par", 2)
     multiply(2)
@@ -279,26 +279,23 @@
     give(3)
     keep(4)
     give(5)
-    keep(3)
     ready(4)
     steps(4, 1)
+    keep(3)
     keep(5)
     ready(3)
     ready(5)
     steps(3, 0)
-    last(2)
-    last(6)
+    for dy in (2, 6, 1, 7, 0):
+        last(dy)
     steps(3, 1)
     ready(2)
     ready(6)
     steps(2, 0)
-    last(1)
-    last(7)
     steps(2, 1)
     ready(1)
     ready(7)
     steps(1, 0)
-    last(0)
     steps(1, 1)
     ready(0)
 

time: 104 us -> 105 us (level)
    pallas_call x1, Pallas kernels: 102 us -> 103 us  [on_device(): pl.pallas_call(kernel, out_shape=jax.ShapeDtypeStruct((1, 1, BLK, BLK), j...]
where the time goes in v7:
time: 105 us
  Pallas kernels  103 us (98%)
  other arithmetic  1.49 us (1%)
    pallas_call x1, Pallas kernels, on_device(): pl.pallas_call(kernel, out_shape=jax.ShapeDtypeStruct((1, 1, BLK, BLK), j...  103 us

profile of v7, /device:TPU:8, one launch (start us, length us, event | category | flops | bytes accessed | tf_op | source)
XLA Modules:
  0.0 104.8 jit_solution(72285085946568775)
XLA Ops:
  0.7 102.7 %shard_map.46 = f32[1,1,128,128]{3,2,1,0:T(8,128)} custom-call(s32[1,2,64]{2,1,0:T(2,128)} %bitcast.3, bf16[1024,512]{1,0:T(8,128)(2,1)} %act.1, bf16[1024,1792]{1,0:T(8,128)(2,1)} %grad.1), custom_call_target="tpu_custom_call" | custom-call | tf_op jit(solution)/shard_map/pallas_call | solution.py:340
  103.3 1.5 %broadcast_select_fusion = f32[1,1,128,128]{3,2,1,0:T(8,128)} fusion(f32[1,1,128,128]{3,2,1,0:T(8,128)} %shard_map.46, pred[]{:T(512)S(6)} %lt.3), kind=kLoop, calls=%fused_computation | loop fusion | flops 16384 | bytes 131073 | tf_op jit(solution)/shard_map/jit(_where)/select_n | solution.py:373

commit v8 on v7

--- a/solution.py
+++ b/solution.py
@@ -223,16 +223,16 @@
     cross(2)
     pass_on("par", 1)
     cross(3)
+    late_hop(3)
     pass_on("par", 2)
-    late_hop(3)
     rest("own", 0)
     rest("par", 0)
     multiply(0)
-    pass_on("par", 3)
-    late_hop(4)
     rest("own", 1)
     rest("par", 1)
     multiply(1)
+    pass_on("par", 3)
+    late_hop(4)
     rest("own", 2)
     rest("par", 2)
     multiply(2)

time: 105 us -> 105 us (level)
  no operation moved by 1% of the time
where the time goes in v8:
time: 105 us
  Pallas kernels  103 us (98%)
  other arithmetic  1.49 us (1%)
    pallas_call x1, Pallas kernels, on_device(): pl.pallas_call(kernel, out_shape=jax.ShapeDtypeStruct((1, 1, BLK, BLK), j...  103 us

profile of v8, /device:TPU:8, one launch (start us, length us, event | category | flops | bytes accessed | tf_op | source)
XLA Modules:
  0.0 104.7 jit_solution(9758754506197632544)
XLA Ops:
  0.7 102.6 %shard_map.46 = f32[1,1,128,128]{3,2,1,0:T(8,128)} custom-call(s32[1,2,64]{2,1,0:T(2,128)} %bitcast.3, bf16[1024,512]{1,0:T(8,128)(2,1)} %act.1, bf16[1024,1792]{1,0:T(8,128)(2,1)} %grad.1), custom_call_target="tpu_custom_call" | custom-call | tf_op jit(solution)/shard_map/pallas_call | solution.py:340
  103.2 1.5 %broadcast_select_fusion = f32[1,1,128,128]{3,2,1,0:T(8,128)} fusion(f32[1,1,128,128]{3,2,1,0:T(8,128)} %shard_map.46, pred[]{:T(512)S(6)} %lt.3), kind=kLoop, calls=%fused_computation | loop fusion | flops 16384 | bytes 131073 | tf_op jit(solution)/shard_map/jit(_where)/select_n | solution.py:373
